TPU v7x, 128 devices: a whole 4x4x4 slice. The times are simulated.
128 devices in a mesh: chan: 8 (over y, core), facet: 16 (over z, x).
Axes of the slice: x: 4, y: 4, z: 4, core: 2. Of those that a mesh axis runs over, the one named last changes fastest.
Arguments:
- visibilities: bfloat16 [32, 8, 8, 65536], P(None, None, 'chan', 'facet'), may hold values from -6 to 6
- w_kernel: bfloat16 [32, 2, 8], replicated, may hold values from -2 to 2
- w_index: int32 [8, 65536], P(None, 'facet'), may hold values from 0 to 31
- cell_offsets: int32 [2, 8, 65536], P(None, None, 'facet'), may hold values from 0 to 24
- block_sub: int32 [8, 128], P(None, 'facet'), may hold values from 0 to 31
- intersection_rows: int32 [16, 32], replicated, may hold values from 0 to 63, as said below
- intersection_count: int32 [16], replicated, may hold values from 1 to 32, as said below
Outputs:
- sky_image: float32 [32, 4, 64, 32768], P('chan', None, None, 'facet')
Inputs may be any that keep to these rules, and one draw needn't show every extreme that they name: `intersection_rows`: the rows in one facet's list are distinct. `intersection_count`: some facet other than the last has exactly 32 entries in use.
All inputs are finite; a program needn't handle non-finite values.
Results may differ from a plain program's by a relative error of at most 0.0059.
Values may be sent and summed in bfloat16 or wider, within the bound.
A program may use at most 128 MiB of HBM per device.

v0:
```python
import math

import jax
import jax.numpy as jnp
from jax import lax
from jax.sharding import PartitionSpec as P

BLK = 512
SG = 32
NSUB = 32
FX = 2048
FY = 64
MARGIN = 128


def shifted(block, axis, distance):
    devices = range(lax.axis_size(axis))
    route = [(i - distance, i) for i in devices if i - distance in devices]
    return lax.ppermute(block, axis, route)


def anchors(sub_index, side_len, period):
    span = period // side_len
    row_anchor = (jnp.mod(sub_index * 37, span) - span // 2) * side_len
    col_anchor = (jnp.mod(sub_index * 53 + 5, span) - span // 2) * side_len
    return (row_anchor, col_anchor)


def row_tables(sub_index, side_len, height, period):
    row_anchor, col_anchor = anchors(sub_index, side_len, period)
    cell_ids = jnp.arange(side_len, dtype=jnp.int32)
    line_ids = jnp.arange(height, dtype=jnp.int32) - height // 2
    phase_int = (row_anchor[:, None, None] + cell_ids[None, None, :]) * line_ids[None, :, None]
    radians = jnp.mod(phase_int, period).astype(jnp.float32) * (2.0 * math.pi / period)
    return (jnp.cos(radians).astype(jnp.bfloat16), jnp.sin(radians).astype(jnp.bfloat16))


def col_tables(sub_index, side_len, col_ids, period):
    row_anchor, col_anchor = anchors(sub_index, side_len, period)
    cell_ids = jnp.arange(side_len, dtype=jnp.int32)
    phase_int = (col_anchor[:, None, None] + cell_ids[None, :, None]) * (col_ids - period // 2)[
        None, None, :
    ]
    radians = jnp.mod(phase_int, period).astype(jnp.float32) * (2.0 * math.pi / period)
    return (jnp.cos(radians).astype(jnp.bfloat16), (-jnp.sin(radians)).astype(jnp.bfloat16))


def place_kernel(values, offsets, side_len):
    distance = jnp.arange(side_len, dtype=jnp.int32)[:, None] - offsets[None, :]
    running = jnp.zeros((values.shape[0], side_len, offsets.shape[0]), jnp.float32)
    for tap_idx in range(values.shape[1]):
        running = (
            running + values[:, tap_idx, None, :] * (distance == tap_idx).astype(jnp.float32)[None]
        )
    return running


def combine(products, side_len, row_width):
    real_part = products[:, :side_len, :row_width] - products[:, side_len:, row_width:]
    imag_part = products[:, :side_len, row_width:] + products[:, side_len:, :row_width]
    return jnp.stack([real_part, imag_part], axis=1)


def block_terms(vis_part, plane_ids, cell_pos, kernel, side_len, block_len):
    planes = kernel.shape[0]
    plane_pick = (jnp.arange(planes, dtype=jnp.int32)[:, None] == plane_ids[None, :]).astype(
        jnp.float32
    )
    values = jnp.einsum(
        "wqk,wr->qkr", kernel.astype(jnp.float32), plane_pick, precision=lax.Precision.HIGHEST
    )
    left_kern = place_kernel(values, cell_pos[0], side_len).astype(jnp.bfloat16)
    right_kern = place_kernel(values, cell_pos[1], side_len)
    num_pols = vis_part.shape[1] // 2
    vis_real = vis_part[:, :num_pols].astype(jnp.float32)[:, :, None, :]
    vis_imag = vis_part[:, num_pols:].astype(jnp.float32)[:, :, None, :]
    y_real = (vis_real * right_kern[0][None, None] - vis_imag * right_kern[1][None, None]).astype(
        jnp.bfloat16
    )
    y_imag = (vis_real * right_kern[1][None, None] + vis_imag * right_kern[0][None, None]).astype(
        jnp.bfloat16
    )
    num_rows = plane_ids.shape[0]
    blocks = num_rows // block_len
    row_width = vis_part.shape[0] * num_pols * side_len
    stacked = jnp.concatenate(
        [
            y_real.reshape(row_width, blocks, block_len),
            y_imag.reshape(row_width, blocks, block_len),
        ],
        axis=0,
    )
    left_flat = left_kern.reshape(2 * side_len, blocks, block_len)
    products = lax.dot_general(
        left_flat, stacked, (((2,), (2,)), ((1,), (1,))), preferred_element_type=jnp.float32
    )
    return combine(products, side_len, row_width)


def to_rows(subgrid, row_cos, row_sin, img_scale):
    sub_real = subgrid[:, 0]
    sub_imag = subgrid[:, 1]

    def apply_table(table, data):
        return jnp.einsum("gyu,guq->gyq", table, data, preferred_element_type=jnp.float32)

    real_part = apply_table(row_cos, sub_real) - apply_table(row_sin, sub_imag)
    imag_part = apply_table(row_cos, sub_imag) + apply_table(row_sin, sub_real)
    return (jnp.stack([real_part, imag_part], axis=1) * img_scale).astype(jnp.bfloat16)


def project(image_sum, row_image, first_sub, col_ids, period):
    num_items = row_image.shape[0]
    group_len = math.gcd(num_items, 8)
    side_len = SG
    mixed = image_sum.shape[0]
    shaped = row_image.reshape(num_items, 2, row_image.shape[2], mixed, side_len)

    def add_group(turn_idx, running):
        row_piece = lax.dynamic_slice_in_dim(shaped, turn_idx * group_len, group_len, 0)
        sub_index = first_sub + turn_idx * group_len + jnp.arange(group_len, dtype=jnp.int32)
        col_cos, col_sin = col_tables(sub_index, side_len, col_ids, period)
        col_table = jnp.stack([col_cos, col_sin], axis=1)
        return running + jnp.einsum(
            "grycv,grvx->cyx", row_piece, col_table, preferred_element_type=jnp.float32
        )

    return lax.fori_loop(0, num_items // group_len, add_group, image_sum)


def shards(
    visibilities, w_kernel, w_index, cell_offsets, block_sub, intersection_rows, intersection_count
):
    turned = lax.all_to_all(visibilities, "chan", split_axis=0, concat_axis=2, tiled=True)
    groups = lax.axis_size("chan")
    facets = lax.axis_size("facet")
    num_chans = turned.shape[0]
    num_pols = turned.shape[1] // 2
    side_len = SG
    per_dev = w_index.shape[1] // BLK
    row_width = num_chans * num_pols * side_len

    def grid_group(group_id):
        vis_part = lax.dynamic_index_in_dim(turned, group_id, 2, keepdims=False)
        plane_ids = lax.dynamic_index_in_dim(w_index, group_id, 0, keepdims=False)
        cell_pos = lax.dynamic_index_in_dim(cell_offsets, group_id, 1, keepdims=False)
        return block_terms(vis_part, plane_ids, cell_pos, w_kernel, side_len, BLK)

    grid_parts = lax.map(grid_group, jnp.arange(groups, dtype=jnp.int32))
    blocks = groups * per_dev
    grid_parts = grid_parts.reshape(blocks, 2 * side_len * row_width)
    sub_ids = block_sub.reshape(blocks)
    plane_pick = (jnp.arange(NSUB, dtype=jnp.int32)[:, None] == sub_ids[None, :]).astype(
        jnp.float32
    )
    img_scale = 1.0 / math.sqrt(groups * facets * w_index.shape[1])
    period = FX * facets
    facet_id = lax.axis_index("facet")
    col_ids = facet_id * FX + jnp.arange(FX, dtype=jnp.int32)
    image = jnp.zeros((num_chans * num_pols, FY, FX), jnp.float32)
    partial_sum = jnp.dot(plane_pick, grid_parts, precision=lax.Precision.HIGHEST)
    summed = lax.psum(partial_sum, "facet")
    subgrid = summed.reshape(NSUB, 2, side_len, row_width).astype(jnp.bfloat16)
    sub_index = jnp.arange(NSUB, dtype=jnp.int32)
    row_cos, row_sin = row_tables(sub_index, side_len, FY, period)
    row_image = to_rows(subgrid, row_cos, row_sin, img_scale)
    image = project(image, row_image, 0, col_ids, period)
    line_ids = jnp.arange(FY, dtype=jnp.int32)
    slot_ids = jnp.arange(intersection_rows.shape[1], dtype=jnp.int32)
    edge_cols = image[:, :, FX - MARGIN :]
    listed = lax.dynamic_index_in_dim(intersection_rows, facet_id, 0, keepdims=False)
    in_use = lax.dynamic_index_in_dim(intersection_count, facet_id, 0, keepdims=False)
    row_keep = jnp.sum(
        ((listed[:, None] == line_ids[None, :]) & (slot_ids[:, None] < in_use)).astype(jnp.float32),
        axis=0,
    )
    arrived = shifted(edge_cols * row_keep[None, :, None], "facet", 1)
    sky_image = jnp.concatenate([image[:, :, :MARGIN] + arrived, image[:, :, MARGIN:]], axis=2)
    return sky_image.reshape(num_chans, num_pols, FY, FX)


def solution(mesh):
    return jax.shard_map(
        shards,
        mesh=mesh,
        in_specs=(
            P(None, None, "chan", "facet"),
            P(),
            P(None, "facet"),
            P(None, None, "facet"),
            P(None, "facet"),
            P(),
            P(),
        ),
        out_specs=P("chan", None, None, "facet"),
        check_vma=False,
    )
```

profile of v0, /device:TPU:0, one launch (start us, length us, event | category | flops | bytes accessed | tf_op | source)
XLA Modules:
  0.0 461.7 jit_solution(6023699204950626542)
XLA Ops:
  0.0 4.7 %all-to-all-start = ((bf16[32,8,1,4096]{3,1,2,0:T(8,128)(2,1)}), bf16[32,8,1,4096]{3,1,2,0:T(8,128)(2,1)S(1)}, u32[]{:S(2)}, u32[]{:S(2)}) async-start(bf16[32,8,1,4096]{3,1,2,0:T(8,128)(2,1)} %param.11), calls=%async_computation | async-start | bytes 4194304 | tf_op jit(solution)/shard_map/all_to_all | solution.py:134
  6.8 25.1 %all-to-all-done = bf16[32,8,1,4096]{3,1,2,0:T(8,128)(2,1)S(1)} async-done(((bf16[32,8,1,4096]{3,1,2,0:T(8,128)(2,1)}), bf16[32,8,1,4096]{3,1,2,0:T(8,128)(2,1)S(1)}, u32[]{:S(2)}, u32[]{:S(2)}) %all-to-all-start) | async-done | bytes 2097184 | tf_op jit(solution)/shard_map/all_to_all | solution.py:134
  31.9 175.5 %while.27 = (s32[]{:T(128)}, f32[8,8,2,32,512]{4,3,2,1,0:T(8,128)}, s32[8]{0:T(128)S(1)}, s32[8,4096]{1,0:T(8,128)}, bf16[32,2,8]{0,2,1:T(8,128)(2,1)S(1)}, /*in...) while((s32[]{:T(128)}, f32[8,8,2,32,512]{4,3,2,1,0:T(8,128)}, ...), condition=%wide.region_1.2_spmd, body=%wide.region_0.1_spmd.sunk | while | flops 587988992 | bytes 84559040 | solution.py:149
  39.5 2.6 subtract_convert_fusion.2
  42.1 2.2 copy.91
  44.3 1.5 copy.92
  45.8 2.2 copy.93
  48.0 1.5 copy.94
  49.5 3.0 fusion.100
  61.4 2.6 subtract_convert_fusion.2
  64.0 2.2 copy.91
  66.3 1.5 copy.92
  67.7 2.2 copy.93
  71.4 3.0 fusion.100
  83.3 2.6 subtract_convert_fusion.2
  86.0 2.2 copy.91
  88.2 1.5 copy.92
  89.7 2.2 copy.93
  93.4 3.0 fusion.100
  105.3 2.6 subtract_convert_fusion.2
  107.9 2.2 copy.91
  110.1 1.5 copy.92
  111.6 2.2 copy.93
  115.3 3.0 fusion.100
  127.2 2.6 subtract_convert_fusion.2
  129.8 2.2 copy.91
  133.5 2.2 copy.93
  137.2 3.0 fusion.100
  149.1 2.6 subtract_convert_fusion.2
  151.8 2.2 copy.91
  155.5 2.2 copy.93
  159.2 3.0 fusion.100
  171.1 2.6 subtract_convert_fusion.2
  173.7 2.2 copy.91
  177.4 2.2 copy.93
  181.1 3.0 fusion.100
  193.0 2.6 subtract_convert_fusion.2
  195.7 2.2 copy.91
  199.4 2.2 copy.93
  203.1 3.0 fusion.100
  207.5 9.4 %reshape.590 = f32[64,32768]{1,0:T(8,128)} reshape(f32[8,8,2,32,512]{4,3,2,1,0:T(8,128)} %get-tuple-element.178) | data formatting | bytes 16777216 | tf_op jit(solution)/shard_map/reshape | solution.py:151
  216.8 8.4 %fusion.60 = f32[32,32768]{1,0:T(8,128)} fusion(f32[64,32768]{1,0:T(8,128)} %reshape.590, s32[64]{0:T(128)S(1)} %eq.182), kind=kOutput, calls=%fused_computation.121 | convolution fusion | flops 805308416 | bytes 12583168 | tf_op jit(solution)/shard_map/dot_general | solution.py:161
  225.2 105.5 %all-reduce.1 = bf16[32,32768]{1,0:T(8,128)(2,1)} all-reduce(f32[32,32768]{1,0:T(8,128)} %fusion.60), channel_id=1, replica_groups=mesh['chan'=8,'facet'=16] {'facet'}, use_global_device_ids=true, to_apply=%region_2.3 | all-reduce | flops 1048576 | bytes 6291456 | tf_op jit(solution)/shard_map/psum | solution.py:162
  330.7 2.3 copy.59
  333.0 2.7 fusion.56
  335.8 4.0 fusion.55
  339.8 4.2 convolution_add_fusion
  344.0 6.8 %copy.38 = f32[32,64,512]{1,2,0:T(8,128)} copy(f32[32,64,512]{2,1,0:T(8,128)} %convolution_add_fusion) | data formatting | bytes 8388608 | tf_op jit(solution)/shard_map/add | solution.py:108
  350.8 5.7 %convolution_subtract_fusion = f32[32,64,512]{2,1,0:T(8,128)} fusion(f32[32,64,512]{2,1,0:T(8,128)} %fusion.55, bf16[32,2,32,512]{3,2,1,0:T(8,128)(2,1)S(1)} %bitcast.145, s32[64]{0:T(128)S(1)} %iota_add_fusion.2, s32[32,32]{1,0:T(8,128)S(1)} %iota_add_fusion.1), kind=kOutput, calls=%fused_computation.100 | convolution fusion | flops 69140480 | bytes 9454080 | tf_op jit(solution)/shard_map/gyu,guq->gyq/dot_general | solution.py:105
  356.6 6.9 %copy.37 = f32[32,64,512]{1,2,0:T(8,128)} copy(f32[32,64,512]{2,1,0:T(8,128)} %convolution_subtract_fusion) | data formatting | bytes 8388608 | tf_op jit(solution)/shard_map/sub | solution.py:107
  363.5 9.8 %fusion.54 = bf16[32,2,64,16,32]{2,4,3,0,1:T(8,128)(2,1)} fusion(f32[32,1,64,16,32]{2,4,3,0,1:T(8,128)} %bitcast.140, f32[32,1,64,16,32]{2,4,3,0,1:T(8,128)} %bitcast.141), kind=kLoop, calls=%fused_computation.97 | loop fusion | flops 6291456 | bytes 12582912 | tf_op jit(solution)/shard_map/convert_element_type | solution.py:109
  373.3 73.2 %while.28 = (s32[]{:T(128)}, f32[16,64,2048]{2,1,0:T(8,128)}, bf16[32,2,64,16,32]{2,4,3,0,1:T(8,128)(2,1)}, s32[]{:T(128)}, s32[]{:T(128)}, /*index=5*/s32[]{:T(128)}, s32[]{:T(128)}, s32[]{:T(128)}) while((s32[]{:T(128)}, f32[16,64,2048]{2,1,0:T(8,128)}, bf16[32,2,64,16,32]{2,4,3,0,1:T(8,128)(2,1)}, s32[]{:T(128)}, s32[]{:T(128)}, ...), condition=%wide.region_4.5_spmd.clone, body=%wide.region_3.4_spmd.clone.sunk | while | flops 2164789760 | bytes 23087328 | solution.py:128
  373.4 8.9 %cosine_convert_fusion.5 = (bf16[8,1,32,2048]{3,2,1,0:T(8,128)(2,1)S(1)}, bf16[8,1,32,2048]{3,2,1,0:T(8,128)(2,1)S(1)}) fusion(s32[2048]{0:T(1024)S(1)} %add_add_fusion.2, s32[8,32]{1,0:T(8,128)S(1)} %iota_add_fusion.4), kind=kLoop, calls=%fused_computation.85.clone.1 | loop fusion | flops 8912896 | bytes 2106368 | tf_op jit(solution)/shard_map/while/body/eval_jaxpr/convert_element_type | solution.py:45
  382.3 7.4 %bitcast_add_fusion.2 = f32[16,64,2048]{2,1,0:T(8,128)} fusion(f32[16,64,2048]{2,1,0:T(8,128)} %get-tuple-element.474, pred[]{:T(512)S(6)} %compare.19, bf16[8,1,32,2048]{3,2,1,0:T(8,128)(2,1)S(1)} %get-tuple-element.430, bf16[8,1,32,2048]{3,2,1,0:T(8,128)(2,1)S(1)} %get-tuple-element.431, bf16[32,2,64,16,32]{2,4,3,0,1:T(8,128)(2,1)} %get-tuple-element.483, ...), kind=kOutput, calls=%fused_computation.71.clone.1 | convolution fusion | flops 2155872256 | bytes 20971524 | tf_op jit(solution)/shard_map/while/body/eval_jaxpr/grycv,grvx->cyx/dot_general | solution.py:124
  389.9 8.9 %cosine_convert_fusion.5 = (bf16[8,1,32,2048]{3,2,1,0:T(8,128)(2,1)S(1)}, bf16[8,1,32,2048]{3,2,1,0:T(8,128)(2,1)S(1)}) fusion(s32[2048]{0:T(1024)S(1)} %add_add_fusion.2, s32[8,32]{1,0:T(8,128)S(1)} %iota_add_fusion.4), kind=kLoop, calls=%fused_computation.85.clone.1 | loop fusion | flops 8912896 | bytes 2106368 | tf_op jit(solution)/shard_map/while/body/eval_jaxpr/convert_element_type | solution.py:45
  398.8 9.9 %bitcast_add_fusion.2 = f32[16,64,2048]{2,1,0:T(8,128)} fusion(f32[16,64,2048]{2,1,0:T(8,128)} %get-tuple-element.474, pred[]{:T(512)S(6)} %compare.19, bf16[8,1,32,2048]{3,2,1,0:T(8,128)(2,1)S(1)} %get-tuple-element.430, bf16[8,1,32,2048]{3,2,1,0:T(8,128)(2,1)S(1)} %get-tuple-element.431, bf16[32,2,64,16,32]{2,4,3,0,1:T(8,128)(2,1)} %get-tuple-element.483, ...), kind=kOutput, calls=%fused_computation.71.clone.1 | convolution fusion | flops 2155872256 | bytes 20971524 | tf_op jit(solution)/shard_map/while/body/eval_jaxpr/grycv,grvx->cyx/dot_general | solution.py:124
  408.8 8.9 %cosine_convert_fusion.5 = (bf16[8,1,32,2048]{3,2,1,0:T(8,128)(2,1)S(1)}, bf16[8,1,32,2048]{3,2,1,0:T(8,128)(2,1)S(1)}) fusion(s32[2048]{0:T(1024)S(1)} %add_add_fusion.2, s32[8,32]{1,0:T(8,128)S(1)} %iota_add_fusion.4), kind=kLoop, calls=%fused_computation.85.clone.1 | loop fusion | flops 8912896 | bytes 2106368 | tf_op jit(solution)/shard_map/while/body/eval_jaxpr/convert_element_type | solution.py:45
  417.7 9.9 %bitcast_add_fusion.2 = f32[16,64,2048]{2,1,0:T(8,128)} fusion(f32[16,64,2048]{2,1,0:T(8,128)} %get-tuple-element.474, pred[]{:T(512)S(6)} %compare.19, bf16[8,1,32,2048]{3,2,1,0:T(8,128)(2,1)S(1)} %get-tuple-element.430, bf16[8,1,32,2048]{3,2,1,0:T(8,128)(2,1)S(1)} %get-tuple-element.431, bf16[32,2,64,16,32]{2,4,3,0,1:T(8,128)(2,1)} %get-tuple-element.483, ...), kind=kOutput, calls=%fused_computation.71.clone.1 | convolution fusion | flops 2155872256 | bytes 20971524 | tf_op jit(solution)/shard_map/while/body/eval_jaxpr/grycv,grvx->cyx/dot_general | solution.py:124
  427.7 8.9 %cosine_convert_fusion.5 = (bf16[8,1,32,2048]{3,2,1,0:T(8,128)(2,1)S(1)}, bf16[8,1,32,2048]{3,2,1,0:T(8,128)(2,1)S(1)}) fusion(s32[2048]{0:T(1024)S(1)} %add_add_fusion.2, s32[8,32]{1,0:T(8,128)S(1)} %iota_add_fusion.4), kind=kLoop, calls=%fused_computation.85.clone.1 | loop fusion | flops 8912896 | bytes 2106368 | tf_op jit(solution)/shard_map/while/body/eval_jaxpr/convert_element_type | solution.py:45
  436.6 9.9 %bitcast_add_fusion.2 = f32[16,64,2048]{2,1,0:T(8,128)} fusion(f32[16,64,2048]{2,1,0:T(8,128)} %get-tuple-element.474, pred[]{:T(512)S(6)} %compare.19, bf16[8,1,32,2048]{3,2,1,0:T(8,128)(2,1)S(1)} %get-tuple-element.430, bf16[8,1,32,2048]{3,2,1,0:T(8,128)(2,1)S(1)} %get-tuple-element.431, bf16[32,2,64,16,32]{2,4,3,0,1:T(8,128)(2,1)} %get-tuple-element.483, ...), kind=kOutput, calls=%fused_computation.71.clone.1 | convolution fusion | flops 2155872256 | bytes 20971524 | tf_op jit(solution)/shard_map/while/body/eval_jaxpr/grycv,grvx->cyx/dot_general | solution.py:124
  447.7 1.6 collective-permute-start
  449.3 3.8 slice.85
  453.1 2.9 collective-permute-done
  457.1 4.6 pad_maximum_fusion
  (200 shorter events, 75.5 us)
Async XLA Ops:
  0.0 6.1 %copy-start = (s32[16,32]{1,0:T(8,128)S(1)}, s32[16,32]{1,0:T(8,128)}, u32[]{:S(2)}) copy-start(s32[16,32]{1,0:T(8,128)} %param.16) | copy-start | bytes 6148
  0.0 4.7 %copy-start.3 = (s32[8,8]{1,0:T(8,128)S(1)}, s32[8,8]{1,0:T(8,128)}, u32[]{:S(2)}) copy-start(s32[8,8]{1,0:T(8,128)} %param.15) | copy-start | bytes 772
  0.0 4.8 %copy-start.5 = (s32[16]{0:T(128)S(1)}, s32[16]{0:T(128)}, u32[]{:S(2)}) copy-start(s32[16]{0:T(128)} %param.17) | copy-start | bytes 196
  0.0 31.9 %copy-start.2 = (bf16[32,2,8]{0,2,1:T(8,128)(2,1)S(1)}, bf16[32,2,8]{0,2,1:T(8,128)(2,1)}, u32[]{:S(2)}) copy-start(bf16[32,2,8]{0,2,1:T(8,128)(2,1)} %param.12) | copy-start | bytes 3076
  0.0 31.9 %all-to-all-start = ((bf16[32,8,1,4096]{3,1,2,0:T(8,128)(2,1)}), bf16[32,8,1,4096]{3,1,2,0:T(8,128)(2,1)S(1)}, u32[]{:S(2)}, u32[]{:S(2)}) async-start(bf16[32,8,1,4096]{3,1,2,0:T(8,128)(2,1)} %param.11), calls=%async_computation | async-start | bytes 4194304 | tf_op jit(solution)/shard_map/all_to_all | solution.py:134
  373.3 73.2 %copy-start.4 = (f32[64]{0:T(128)S(1)}, f32[64]{0:T(128)}, u32[]{:S(2)}) copy-start(f32[64]{0:T(128)} %convert_reduce_fusion) | copy-start | bytes 772
  447.7 8.3 %collective-permute-start = (f32[16,64,128]{2,1,0:T(8,128)S(1)}, f32[16,64,128]{2,1,0:T(8,128)S(1)}, u32[]{:S(2)}, u32[]{:S(2)}) collective-permute-start(f32[16,64,128]{2,1,0:T(8,128)S(1)} %slice_multiply_fusion), channel_id=1, source_target_pairs={{0,1},{1,2},{2,3},{3,4},{4,5},{5,6},{6,7},{7,8},{8,9},{9,10},{10,1... | collective-permute-start | bytes 1572872 | tf_op jit(solution)/shard_map/ppermute | solution.py:19
  457.1 4.6 copy-start.1
where the time goes:
time: 464 us; the launch traced here: 462 us
  local copies, waits for them, and re-layouts  115 us (25%)
  blocking collectives  105 us (23%)
  other arithmetic  102 us (22%)
  matrix products  88.1 us (19%)
  waiting for transfers between devices  28 us (6%)
  loops' own time  16.5 us (4%)
  starting transfers between devices  6.35 us (1%)
    psum x1, blocking collectives, shards(): summed = lax.psum(partial_sum, 'facet')  105 us
    while x56, local copies, waits for them, and re-layouts  38.8 us
    dot_general x4, matrix products, add_group(): jnp.einsum('grycv,grvx->cyx', row_piece, col_table, preferred_element_typ...  37.1 us
    convert_element_type x4, other arithmetic, col_tables(): jnp.cos(radians).astype(jnp.bfloat16)  35.7 us
    all_to_all x1, waiting for transfers between devices, shards(): lax.all_to_all(visibilities, 'chan', split_axis=0, concat_axis=2, tiled=T...  25.1 us
    dot_general x8, matrix products, block_terms(): lax.dot_general(left_flat, stacked, (((2,), (2,)), ((1,), (1,))), preferr...  24.4 us
    convert_element_type x8, other arithmetic, block_terms(): (vis_real * right_kern[0][None, None] - vis_imag * right_kern[1][None, No...  21 us
    dot_general x4, matrix products, apply_table(): jnp.einsum('gyu,guq->gyq', table, data, preferred_element_type=jnp.float32)  16.7 us
  transfers between devices with their start and end apart: 2, of which 2 were waited for; matrix products, arithmetic and copies ran while one was open for 1% of the time, Pallas kernels for 0%

commit v1 on v0

v1 whole, which is shorter than its diff:
```python
import math

import jax
import jax.numpy as jnp
import numpy as np
from jax import lax
from jax.experimental import pallas as pl
from jax.experimental.pallas import tpu as pltpu
from jax.sharding import PartitionSpec as P

BLK = 512
SG = 32
NSUB = 32
FX = 2048
FY = 64
MARGIN = 128
NX = 32768
GROUPS = 8
NB = 64
CH = 4
POL = 4
STAGES = 2
CPS = CH // STAGES
NL = CPS * POL * SG
RING = 4
BF = jnp.bfloat16
F32 = jnp.float32
MESH = pl.DeviceIdType.MESH


def sort_plan(block_sub):
    sub = block_sub.reshape(NB)
    ids = jnp.arange(NB, dtype=jnp.int32)
    before = (sub[None, :] < sub[:, None]) | (
        (sub[None, :] == sub[:, None]) & (ids[None, :] < ids[:, None])
    )
    rank = jnp.sum(before.astype(jnp.int32), axis=1)
    hit = rank[None, :] == ids[:, None]
    order = jnp.sum(jnp.where(hit, ids[None, :], 0), axis=1)
    placed = jnp.sum(jnp.where(hit, sub[None, :], 0), axis=1)
    same = jnp.concatenate([jnp.zeros((1,), jnp.bool_), placed[1:] == placed[:-1]])
    want = jnp.arange(NSUB, dtype=jnp.int32)[:, None]
    last = jnp.maximum(jnp.sum((sub[None, :] <= want).astype(jnp.int32), axis=1) - 1, 0)
    has = jnp.any(sub[None, :] == want, axis=1)
    return order, same.astype(F32), last, has.astype(F32)


def gather_kernel(
    vis,
    widx_h,
    offs_h,
    table,
    order,
    same,
    last,
    has,
    grid_out,
    *scratch,
):
    recv = scratch[:STAGES]
    (
        widx,
        offs,
        left,
        right,
        pref,
        part,
        in1,
        mid,
        in2,
        local_sem,
        turn_send,
        turn_recv,
        own_sem,
        ring_send,
        ring_recv,
    ) = scratch[STAGES:]
    me = lax.axis_index("chan")
    facet = lax.axis_index("facet")
    mz = lax.div(facet, RING)
    mx = lax.rem(facet, RING)

    def x_peer(k):
        return lax.rem(mx + k, RING)

    def z_peer(k):
        return lax.rem(mz + k, RING)

    def on_x(x):
        return {"facet": mz * 4 + x}

    def on_z(z):
        return {"facet": z * 4 + mx}

    load_w = pltpu.make_async_copy(widx_h, widx, local_sem.at[0])
    load_o = pltpu.make_async_copy(offs_h, offs, local_sem.at[1])
    load_w.start()
    load_o.start()

    def block_refs(dest, source, st, blk):
        src = vis.at[pl.ds(dest * CH + st * CPS, CPS), :, pl.ds(blk * BLK, BLK)]
        return src, recv[st].at[source * 8 + blk]

    def slab(source, st):
        return recv[st].at[pl.ds(source * 8, 8)]

    for st in range(STAGES):
        for blk in range(8):
            src, dst = block_refs(me, me, st, blk)
            pltpu.make_async_copy(src, dst, own_sem.at[st]).start()

    barrier = pltpu.get_barrier_semaphore()
    for k in range(1, GROUPS):
        peer = lax.rem(me + k, GROUPS)
        pl.semaphore_signal(barrier, inc=1, device_id={"chan": peer}, device_id_type=MESH)
    for k in range(1, RING):
        pl.semaphore_signal(barrier, inc=1, device_id=on_x(x_peer(k)), device_id_type=MESH)
        pl.semaphore_signal(barrier, inc=1, device_id=on_z(z_peer(k)), device_id_type=MESH)
    pl.semaphore_wait(barrier, GROUPS - 1 + 2 * (RING - 1))

    for st in range(STAGES):
        for k in range(1, GROUPS):
            peer = lax.rem(me + k, GROUPS)
            for blk in range(8):
                src, dst = block_refs(peer, me, st, blk)
                pltpu.make_async_remote_copy(
                    src_ref=src,
                    dst_ref=dst,
                    send_sem=turn_send.at[st, k - 1],
                    recv_sem=turn_recv.at[st, k - 1],
                    device_id={"chan": peer},
                    device_id_type=MESH,
                ).start()

    def turned(st):
        mine = slab(me, st)
        pltpu.make_async_copy(mine, mine, own_sem.at[st]).wait()
        for k in range(1, GROUPS):
            peer = lax.rem(me + GROUPS - k, GROUPS)
            got = slab(peer, st)
            pltpu.make_async_remote_copy(
                src_ref=got,
                dst_ref=got,
                send_sem=turn_send.at[st, k - 1],
                recv_sem=turn_recv.at[st, k - 1],
                device_id={"chan": peer},
                device_id_type=MESH,
            ).wait()

    load_w.wait()
    load_o.wait()

    iota8 = lax.broadcasted_iota(jnp.int32, (8, 128), 0)
    tab_re = table[0]
    tab_im = table[1]

    def prep(tile, carry):
        lanes = pl.ds(pl.multiple_of(tile * 128, 128), 128)
        blk = lax.div(tile, 4)
        col = lax.rem(tile, 4) * 128
        cols = pl.ds(pl.multiple_of(col, 128), 128)
        cols_im = pl.ds(pl.multiple_of(col + BLK, 128), 128)
        planes = widx[:, lanes]
        offset = (offs[0, :, lanes], offs[1, :, lanes])
        for g in range(GROUPS):
            b = g * 8 + blk
            plane = jnp.broadcast_to(planes[g : g + 1], (8, 128))
            val_re = jnp.take_along_axis(tab_re, plane, axis=1)
            val_im = jnp.take_along_axis(tab_im, plane, axis=1)
            for side in range(2):
                off = jnp.broadcast_to(offset[side][g : g + 1], (8, 128))
                dist = iota8 - off
                cyc = lax.bitwise_and(dist, 7)
                tap_re = jnp.take_along_axis(val_re, cyc, axis=0)
                tap_im = jnp.take_along_axis(val_im, cyc, axis=0)
                res, ims = [], []
                for q in range(SG // 8):
                    ok = lax.bitwise_and(dist + 8 * q, -8) == 0
                    res.append(jnp.where(ok, tap_re, 0.0))
                    ims.append(jnp.where(ok, tap_im, 0.0))
                k_re = jnp.concatenate(res, axis=0)
                k_im = jnp.concatenate(ims, axis=0)
                if side == 0:
                    re16 = k_re.astype(BF)
                    left[b, 0:SG, cols] = re16
                    left[b, 0:SG, cols_im] = (-k_im).astype(BF)
                    left[b, SG : 2 * SG, cols] = k_im.astype(BF)
                    left[b, SG : 2 * SG, cols_im] = re16
                else:
                    right[b, 0, :, cols] = k_re
                    right[b, 1, :, cols] = k_im
        return carry

    lax.fori_loop(0, GROUPS * BLK // 128, prep, 0)

    def grid_part(st, lo, hi, run):
        def body(j, run):
            b = order[j]
            kern = right[b]
            k_re = kern[0]
            k_im = kern[1]
            seen = recv[st][b]
            rows = []
            for c in range(CPS):
                v = seen[c].astype(F32)
                for p in range(POL):
                    v_re = jnp.broadcast_to(v[p : p + 1], (SG, BLK))
                    v_im = jnp.broadcast_to(v[p + POL : p + POL + 1], (SG, BLK))
                    y_re = (v_re * k_re - v_im * k_im).astype(BF)
                    y_im = (v_re * k_im + v_im * k_re).astype(BF)
                    rows.append(jnp.concatenate([y_re, y_im], axis=1))
            y = jnp.concatenate(rows, axis=0)
            o = lax.dot_general(
                left[b], y, (((1,), (1,)), ((), ())), preferred_element_type=F32
            )
            run = run * same[j] + o
            pref[j] = run
            return run

        return lax.fori_loop(lo, hi, body, run, unroll=4)

    def emit(st):
        def body(s, carry):
            part[st, s] = (pref[last[s]] * has[s]).astype(BF)
            return carry

        lax.fori_loop(0, NSUB, body, 0)

    def ring_copy(st, half, phase, k, src, dst, dev):
        return pltpu.make_async_remote_copy(
            src_ref=src,
            dst_ref=dst,
            send_sem=ring_send.at[st, half, phase, k - 1],
            recv_sem=ring_recv.at[st, half, phase, k - 1],
            device_id=dev,
            device_id_type=MESH,
        )

    copies = {}
    half_n = NSUB // 2
    first = (mx, mz)
    second = (mz, mx)

    def dev_of(half, phase_axis, k):
        along_x = (half == 0) == (phase_axis == 0)
        return (x_peer(k), on_x(x_peer(k))) if along_x else (z_peer(k), on_z(z_peer(k)))

    def rs1(st):
        for half in range(2):
            for k in range(1, RING):
                pos, dev = dev_of(half, 0, k)
                cp = ring_copy(
                    st,
                    half,
                    0,
                    k,
                    part.at[st, pl.ds(half * half_n + 4 * pos, 4)],
                    in1.at[st, half, k - 1],
                    dev,
                )
                cp.start()
                copies[st, half, 0, k] = cp

    def rs2(st):
        for half in range(2):
            for k in range(1, RING):
                copies[st, half, 0, k].wait()
            total = part[st, pl.ds(half * half_n + 4 * first[half], 4)].astype(F32)
            for k in range(1, RING):
                total = total + in1[st, half, k - 1].astype(F32)
            mid[st, half] = total.astype(BF)
            for k in range(1, RING):
                pos, dev = dev_of(half, 1, k)
                cp = ring_copy(st, half, 1, k, mid.at[st, half, pos], in2.at[st, half, k - 1], dev)
                cp.start()
                copies[st, half, 1, k] = cp

    def ag1(st):
        for half in range(2):
            for k in range(1, RING):
                copies[st, half, 1, k].wait()
            total = mid[st, half, second[half]].astype(F32)
            for k in range(1, RING):
                total = total + in2[st, half, k - 1].astype(F32)
            slot = half * half_n + 4 * first[half] + second[half]
            grid_out[st, slot] = total.astype(BF)
            for k in range(1, RING):
                pos, dev = dev_of(half, 1, k)
                cp = ring_copy(
                    st, half, 2, k, grid_out.at[st, slot], grid_out.at[st, slot], dev
                )
                cp.start()
                copies[st, half, 2, k] = cp

    def ag2(st):
        for half in range(2):
            for k in range(1, RING):
                copies[st, half, 2, k].wait()
            span = pl.ds(half * half_n + 4 * first[half], 4)
            for k in range(1, RING):
                pos, dev = dev_of(half, 0, k)
                cp = ring_copy(
                    st, half, 3, k, grid_out.at[st, span], grid_out.at[st, span], dev
                )
                cp.start()
                copies[st, half, 3, k] = cp

    def finish(st):
        for half in range(2):
            for k in range(1, RING):
                copies[st, half, 3, k].wait()

    steps = []
    for st in range(STAGES):
        turned(st)
        run = jnp.zeros((2 * SG, NL), F32)
        for piece in range(4):
            run = grid_part(st, piece * (NB // 4), (piece + 1) * (NB // 4), run)
            if steps:
                steps.pop(0)()
        emit(st)
        rs1(st)
        steps += [
            (lambda st=st: rs2(st)),
            (lambda st=st: ag1(st)),
            (lambda st=st: ag2(st)),
            (lambda st=st: finish(st)),
        ]
    for step in steps:
        step()


def gridded(vis, w_index, offsets, table, plan):
    any_spec = pl.BlockSpec(memory_space=pl.ANY)
    vmem = pl.BlockSpec(memory_space=pltpu.VMEM)
    smem = pl.BlockSpec(memory_space=pltpu.SMEM)
    return pl.pallas_call(
        gather_kernel,
        out_shape=jax.ShapeDtypeStruct((STAGES, NSUB, 2 * SG, NL), BF),
        in_specs=[any_spec, any_spec, any_spec, vmem, smem, smem, smem, smem],
        out_specs=vmem,
        scratch_shapes=[
            *[pltpu.VMEM((NB, CPS, 2 * POL, BLK), BF)] * STAGES,
            pltpu.VMEM((GROUPS, GROUPS * BLK), jnp.int32),
            pltpu.VMEM((2, GROUPS, GROUPS * BLK), jnp.int32),
            pltpu.VMEM((NB, 2 * SG, 2 * BLK), BF),
            pltpu.VMEM((NB, 2, SG, BLK), F32),
            pltpu.VMEM((NB, 2 * SG, NL), F32),
            pltpu.VMEM((STAGES, NSUB, 2 * SG, NL), BF),
            pltpu.VMEM((STAGES, 2, RING - 1, 4, 2 * SG, NL), BF),
            pltpu.VMEM((STAGES, 2, 4, 2 * SG, NL), BF),
            pltpu.VMEM((STAGES, 2, RING - 1, 2 * SG, NL), BF),
            pltpu.SemaphoreType.DMA((2,)),
            pltpu.SemaphoreType.DMA((STAGES, GROUPS - 1)),
            pltpu.SemaphoreType.DMA((STAGES, GROUPS - 1)),
            pltpu.SemaphoreType.DMA((STAGES,)),
            pltpu.SemaphoreType.DMA((STAGES, 2, 4, RING - 1)),
            pltpu.SemaphoreType.DMA((STAGES, 2, 4, RING - 1)),
        ],
        compiler_params=pltpu.CompilerParams(
            collective_id=0, has_side_effects=True, vmem_limit_bytes=60 * 2**20
        ),
        name="turn_grid_share",
    )(vis, w_index, offsets, table, *plan)


XT = 256
NT = FX // XT


def image_kernel(grids, row_tab, e_cos, e_sin, w_cos, w_sin, keep, out, z, col, edge, cur):
    step = pl.program_id(0)
    kblk = 128

    def rotate(q):
        rows = pl.ds(q * kblk, kblk)
        c = cur[0, rows]
        s = cur[1, rows]
        wc = w_cos[rows]
        ws = w_sin[rows]
        cur[0, rows] = c * wc - s * ws
        cur[1, rows] = s * wc + c * ws
        return c, s

    def fill(width):
        for q in range(NSUB * SG // kblk):
            for h in range(width // 128):
                c, s = rotate(q)
                col[pl.ds(q * 2 * kblk, kblk), pl.ds(h * 128, 128)] = c.astype(BF)
                col[pl.ds(q * 2 * kblk + kblk, kblk), pl.ds(h * 128, 128)] = (-s).astype(BF)

    @pl.when(step == 0)
    def _():
        img_scale = 1.0 / math.sqrt(GROUPS * 65536)

        def rows4(q, carry):
            for st in range(STAGES):
                os = []
                for gi in range(4):
                    g = q * 4 + gi
                    os.append(
                        jnp.dot(row_tab[g], grids[st, g], preferred_element_type=F32) * img_scale
                    )
                for c in range(CPS):
                    for p in range(POL):
                        lo = c * POL * SG + p * SG
                        both = jnp.concatenate([o[:, lo : lo + SG] for o in os], axis=1).astype(BF)
                        base = (st * CPS + c) * POL * FY + p * FY
                        lanes0 = pl.ds(pl.multiple_of(q * 256, 128), 128)
                        lanes1 = pl.ds(pl.multiple_of(q * 256 + 128, 128), 128)
                        z[pl.ds(base, FY), lanes0] = both[:FY]
                        z[pl.ds(base, FY), lanes1] = both[FY:]
            return carry

        lax.fori_loop(0, NSUB // 4, rows4, 0)
        cur[0] = e_cos[...]
        cur[1] = e_sin[...]
        fill(128)
        prev = jnp.dot(z[...], col[:, 0:128], preferred_element_type=F32)
        edge[...] = prev * keep[...]

    fill(XT)
    o = jnp.dot(z[...], col[...], preferred_element_type=F32)
    out[...] = o.reshape(CH, POL, FY, XT)

    @pl.when(step == 0)
    def _():
        out[:, :, :, 0:MARGIN] = out[:, :, :, 0:MARGIN] + edge[...].reshape(CH, POL, FY, MARGIN)


def imaged(grids, row_tab, e_cos, e_sin, w_cos, w_sin, keep):
    def whole(shape):
        return pl.BlockSpec(shape, lambda n: (0,) * len(shape), pipeline_mode=pl.Buffered(1))

    return pl.pallas_call(
        image_kernel,
        grid=(NT,),
        out_shape=jax.ShapeDtypeStruct((CH, POL, FY, FX), F32),
        in_specs=[
            whole(a.shape) for a in (grids, row_tab, e_cos, e_sin, w_cos, w_sin, keep)
        ],
        out_specs=pl.BlockSpec((CH, POL, FY, XT), lambda n: (0, 0, 0, n)),
        scratch_shapes=[
            pltpu.VMEM((CH * POL * FY, NSUB * SG * 2), BF),
            pltpu.VMEM((NSUB * SG * 2, XT), BF),
            pltpu.VMEM((CH * POL * FY, MARGIN), F32),
            pltpu.VMEM((2, NSUB * SG, 128), F32),
        ],
        compiler_params=pltpu.CompilerParams(vmem_limit_bytes=60 * 2**20),
        name="facet_image",
    )(grids, row_tab, e_cos, e_sin, w_cos, w_sin, keep)


def row_table():
    g = np.arange(NSUB)
    span = NX // SG
    anchor = ((37 * g) % span - span // 2) * SG
    lines = np.arange(FY) - FY // 2
    phase = ((anchor[:, None, None] + np.arange(SG)[None, None, :]) * lines[None, :, None]) % NX
    rad = phase.astype(np.float32) * np.float32(2.0 * math.pi / NX)
    cos, sin = np.cos(rad), np.sin(rad)
    top = np.concatenate([cos, -sin], axis=2)
    low = np.concatenate([sin, cos], axis=2)
    return np.concatenate([top, low], axis=1)


def shards(
    visibilities, w_kernel, w_index, cell_offsets, block_sub, intersection_rows, intersection_count
):
    facet = lax.axis_index("facet")
    vis = visibilities.reshape(visibilities.shape[0], 2 * POL, w_index.shape[1])
    table = jnp.pad(
        w_kernel.astype(F32).transpose(1, 2, 0), ((0, 0), (0, 0), (0, 128 - w_kernel.shape[0]))
    )
    grids = gridded(vis, w_index, cell_offsets, table, sort_plan(block_sub))

    g = np.arange(NSUB)
    span = NX // SG
    anchor = ((53 * g + 5) % span - span // 2) * SG
    freq = jnp.asarray((anchor[:, None] + np.arange(SG)[None, :]).reshape(-1, 1), jnp.int32)
    start = facet * FX - NX // 2 - MARGIN
    cols = start + jnp.arange(128, dtype=jnp.int32)[None, :]
    to_rad = 2.0 * math.pi / NX
    rad = jnp.mod(freq * cols, NX).astype(F32) * to_rad
    turn = jnp.broadcast_to(jnp.mod(freq * 128, NX).astype(F32) * to_rad, rad.shape)

    before = jnp.maximum(facet - 1, 0)
    listed = lax.dynamic_index_in_dim(intersection_rows, before, 0, keepdims=False)
    in_use = lax.dynamic_index_in_dim(intersection_count, before, 0, keepdims=False)
    slots = jnp.arange(intersection_rows.shape[1], dtype=jnp.int32)
    lines = jnp.arange(FY, dtype=jnp.int32)
    row_keep = jnp.sum(
        ((listed[:, None] == lines[None, :]) & (slots[:, None] < in_use)).astype(F32), axis=0
    ) * (facet > 0).astype(F32)
    keep = jnp.broadcast_to(row_keep[None, :, None], (CH * POL, FY, MARGIN)).reshape(-1, MARGIN)

    return imaged(
        grids,
        jnp.asarray(row_table(), BF),
        jnp.cos(rad),
        jnp.sin(rad),
        jnp.cos(turn),
        jnp.sin(turn),
        keep,
    )


def solution(mesh):
    return jax.shard_map(
        shards,
        mesh=mesh,
        in_specs=(
            P(None, None, "chan", "facet"),
            P(),
            P(None, "facet"),
            P(None, None, "facet"),
            P(None, "facet"),
            P(),
            P(),
        ),
        out_specs=P("chan", None, None, "facet"),
        check_vma=False,
    )
```

time: 464 us -> 120 us (0.26)
  local copies, waits for them, and re-layouts: 115 us -> 5.11 us
  Pallas kernels: 0 us -> 106 us
  blocking collectives: 105 us -> 0 us
  other arithmetic: 102 us -> 8.84 us
  matrix products: 88.1 us -> 0 us
  waiting for transfers between devices: 28 us -> 0 us
  loops' own time: 16.5 us -> 0 us
  starting transfers between devices: 6.35 us -> 0 us
    pallas_call x0 -> x2, Pallas kernels: none -> 106 us  [the longest x1 83.5 us: gridded(): pl.pallas_call(gather_kernel, out_shape=jax.ShapeDtypeStruct((STAGES, NSU...]
    psum x1 -> x0, blocking collectives: 105 us -> none  [shards(): summed = lax.psum(partial_sum, 'facet')]
    dot_general x17 -> x0, matrix products: 86.5 us -> none  [the longest x4 37.1 us: add_group(): jnp.einsum('grycv,grvx->cyx', row_piece, col_table, preferred_element_typ...]
    convert_element_type x45 -> x2, other arithmetic: 79.1 us -> 1.2 us  [sort_plan(): return (order, same.astype(F32), last, has.astype(F32))]
    while x56 -> x0, local copies, waits for them, and re-layouts: 38.8 us -> none
    all_to_all x1 -> x0, waiting for transfers between devices: 25.1 us -> none  [shards(): lax.all_to_all(visibilities, 'chan', split_axis=0, concat_axis=2, tiled=T...]
    convert_element_type x16 -> x0, local copies, waits for them, and re-layouts: 23.3 us -> none  [the longest x8 11.7 us: block_terms(): (vis_real * right_kern[1][None, None] + vis_imag * right_kern[0][None, No...]
    another operation x2 -> x0, loops' own time: 16.5 us -> none  [the longest x1 16.4 us: shards(): grid_parts = lax.map(grid_group, jnp.arange(groups, dtype=jnp.int32))]
  transfers between devices with their start and end apart: 2 -> 0, of which waited for: 2 -> 0; matrix products, arithmetic and copies ran while one was open for 1% -> 0% of each run, Pallas kernels for 0% -> 0%
where the time goes in v1:
time: 120 us
  Pallas kernels  106 us (88%)
  other arithmetic  8.84 us (7%)
  local copies, waits for them, and re-layouts  5.11 us (4%)
    pallas_call x1, Pallas kernels, gridded(): pl.pallas_call(gather_kernel, out_shape=jax.ShapeDtypeStruct((STAGES, NSU...  83.5 us
    pallas_call x1, Pallas kernels, imaged(): pl.pallas_call(image_kernel, grid=(NT,), out_shape=jax.ShapeDtypeStruct((...  22.4 us
    sin x1, other arithmetic, shards(): jnp.sin(rad)  3.9 us

profile of v1, /device:TPU:0, one launch (start us, length us, event | category | flops | bytes accessed | tf_op | source)
XLA Modules:
  0.0 119.9 jit_solution(14297700702529305757)
XLA Ops:
  0.0 0.0 copy-start
  0.0 1.2 %dynamic_slice.9 = s32[1]{0:T(128)} dynamic-slice(s32[16]{0:T(128)} %param.15, s32[]{:T(128)S(6)} %max.11), dynamic_slice_sizes={1} | dynamic-slice | bytes 12 | tf_op jit(solution)/shard_map/jit(dynamic_index_in_dim)/dynamic_slice | solution.py:489
  1.3 0.6 iota_compare_fusion.5
  1.9 0.0 copy-done
  1.9 0.1 convert_reduce_fusion.1
  2.0 0.8 lt.59
  2.8 0.1 fusion.7
  2.9 0.5 convert_element_type.30.has
  3.5 0.1 convert_reduce_fusion.2
  3.6 0.6 add_maximum_fusion.last
  4.2 0.2 convert_reduce_fusion
  4.3 0.6 select_reduce_fusion
  5.0 0.1 slice_compare_fusion
  5.0 0.7 add_convert_fusion.same
  5.7 0.1 broadcast_in_dim.45
  5.8 1.3 %pad_convert_fusion.table = f32[2,8,128]{2,1,0:T(8,128)} fusion(bf16[2,8,32]{2,1,0:T(8,128)(2,1)} %bitcast.6), kind=kLoop, calls=%fused_computation.24 | loop fusion | flops 2048 | bytes 9216 | tf_op jit(solution)/shard_map/jit(_pad)/pad | solution.py:472
  7.1 1.0 broadcast_in_dim.46.keep
  8.1 3.9 %fusion.3 = (f32[1024,128]{1,0:T(8,128)}, f32[1024,128]{1,0:T(8,128)}) fusion(s32[128]{0:T(128)S(1)} %iota_add_fusion, s32[1024]{0:T(1024)} %constant.75), kind=kLoop, calls=%fused_computation.8 | loop fusion | flops 1835008 | bytes 1053184 | tf_op jit(solution)/shard_map/sin | solution.py:501
  12.0 0.0 copy-start.2
  12.0 0.0 copy-start.1
  12.0 83.5 %turn_grid_share.1.grids = bf16[2,32,64,256]{3,2,1,0:T(8,128)(2,1)} custom-call(bf16[32,8,4096]{2,1,0:T(8,128)(2,1)} %bitcast.5, s32[8,4096]{1,0:T(8,128)} %widx_h.1, s32[2,8,4096]{2,1,0:T(8,128)} %offs_h.1, f32[2,8,128]{2,1,0:T(8,128)} %pad_convert_fusion.table, s32[64]{0:T(128)} %get-tuple-element.6.order, f32[64]{0:T(128)} %add_convert_fusion.same, ...), custom_call_target="tpu_custom_call" | custom-call | tf_op jit(solution)/shard_map/turn_grid_share/pallas_call | solution.py:337
  95.5 0.0 copy-done.2
  95.5 1.0 broadcast_in_dim.42.w_cos
  96.6 0.0 copy-done.1
  96.6 1.0 broadcast_in_dim.43.w_sin
  97.6 22.4 %facet_image.1 = f32[4,4,64,2048]{3,2,1,0:T(8,128)} custom-call(bf16[2,32,64,256]{3,2,1,0:T(8,128)(2,1)} %turn_grid_share.1.grids, bf16[32,128,64]{2,1,0:T(8,128)(2,1)} %constant.70.clone.row_tab, f32[1024,128]{1,0:T(8,128)} %get-tuple-element.8.e_cos, f32[1024,128]{1,0:T(8,128)} %get-tuple-element.7.e_sin, f32[1024,128]{1,0:T(8,128)} %broadcast_in_dim.42.w_cos, ...), custom_call_target="tpu_custom_call" | custom-call | tf_op jit(solution)/shard_map/facet_image/pallas_call | solution.py:435
  (4 shorter events, 0.0 us)
Async XLA Ops:
  0.0 1.9 %copy-start = (s32[16,32]{1,0:T(8,128)S(1)}, s32[16,32]{1,0:T(8,128)}, u32[]{:S(2)}) copy-start(s32[16,32]{1,0:T(8,128)} %param.14) | copy-start | bytes 6148
  12.0 83.6 %copy-start.2 = (f32[1024]{0:T(1024)S(1)}, f32[1024]{0:T(1024)}, u32[]{:S(2)}) copy-start(f32[1024]{0:T(1024)} %constant.91) | copy-start | bytes 12292
  12.0 84.6 %copy-start.1 = (f32[1024]{0:T(1024)S(1)}, f32[1024]{0:T(1024)}, u32[]{:S(2)}) copy-start(f32[1024]{0:T(1024)} %constant.93) | copy-start | bytes 12292

commit v2 on v1

--- a/solution.py
+++ b/solution.py
@@ -28,21 +28,39 @@
 MESH = pl.DeviceIdType.MESH
 
 
+def plan_kernel(sub, out):
+    lane = lax.broadcasted_iota(jnp.int32, (NB, 128), 1)
+    line = lax.broadcasted_iota(jnp.int32, (NB, 128), 0)
+    across = jnp.full((NB, 128), NSUB, jnp.int32)
+    down = jnp.zeros((NB, 128), jnp.int32)
+    for b in range(NB):
+        value = sub[b // 8, b % 8]
+        across = jnp.where(lane == b, value, across)
+        down = jnp.where(line == b, value, down)
+    ahead = (across < down) | ((across == down) & (lane < line))
+    rank = jnp.sum(ahead.astype(jnp.int32), axis=1, keepdims=True)
+    hit = rank == lane
+
+    def total(x):
+        return jnp.sum(x.astype(jnp.int32), axis=0, keepdims=True)
+
+    order = total(jnp.where(hit, line, 0))
+    placed = total(jnp.where(hit, down, 0))
+    last = jnp.maximum(total(down <= lane) - 1, 0)
+    has = jnp.minimum(total(down == lane), 1)
+    earlier = pltpu.roll(jnp.broadcast_to(placed, (8, 128)), 1, 1)
+    same = ((earlier[:1] == placed) & (lane[:1] > 0)).astype(jnp.int32)
+    out[...] = jnp.concatenate([order, same, last, has] + [order] * 4, axis=0)
+
+
 def sort_plan(block_sub):
-    sub = block_sub.reshape(NB)
-    ids = jnp.arange(NB, dtype=jnp.int32)
-    before = (sub[None, :] < sub[:, None]) | (
-        (sub[None, :] == sub[:, None]) & (ids[None, :] < ids[:, None])
-    )
-    rank = jnp.sum(before.astype(jnp.int32), axis=1)
-    hit = rank[None, :] == ids[:, None]
-    order = jnp.sum(jnp.where(hit, ids[None, :], 0), axis=1)
-    placed = jnp.sum(jnp.where(hit, sub[None, :], 0), axis=1)
-    same = jnp.concatenate([jnp.zeros((1,), jnp.bool_), placed[1:] == placed[:-1]])
-    want = jnp.arange(NSUB, dtype=jnp.int32)[:, None]
-    last = jnp.maximum(jnp.sum((sub[None, :] <= want).astype(jnp.int32), axis=1) - 1, 0)
-    has = jnp.any(sub[None, :] == want, axis=1)
-    return order, same.astype(F32), last, has.astype(F32)
+    return pl.pallas_call(
+        plan_kernel,
+        out_shape=jax.ShapeDtypeStruct((8, 128), jnp.int32),
+        in_specs=[pl.BlockSpec(memory_space=pltpu.SMEM)],
+        out_specs=pl.BlockSpec(memory_space=pltpu.VMEM),
+        name="sort_plan",
+    )(block_sub)
 
 
 def gather_kernel(
@@ -50,10 +68,7 @@
     widx_h,
     offs_h,
     table,
-    order,
-    same,
-    last,
-    has,
+    plan,
     grid_out,
     *scratch,
 ):
@@ -151,8 +166,9 @@
     load_o.wait()
 
     iota8 = lax.broadcasted_iota(jnp.int32, (8, 128), 0)
-    tab_re = table[0]
-    tab_im = table[1]
+    blank = jnp.zeros((8, 128 - table.shape[2]), F32)
+    tab_re = jnp.concatenate([table[0].astype(F32), blank], axis=1)
+    tab_im = jnp.concatenate([table[1].astype(F32), blank], axis=1)
 
     def prep(tile, carry):
         lanes = pl.ds(pl.multiple_of(tile * 128, 128), 128)
@@ -195,7 +211,7 @@
 
     def grid_part(st, lo, hi, run):
         def body(j, run):
-            b = order[j]
+            b = plan[0, j]
             kern = right[b]
             k_re = kern[0]
             k_im = kern[1]
@@ -213,7 +229,7 @@
             o = lax.dot_general(
                 left[b], y, (((1,), (1,)), ((), ())), preferred_element_type=F32
             )
-            run = run * same[j] + o
+            run = run * plan[1, j].astype(F32) + o
             pref[j] = run
             return run
 
@@ -221,7 +237,7 @@
 
     def emit(st):
         def body(s, carry):
-            part[st, s] = (pref[last[s]] * has[s]).astype(BF)
+            part[st, s] = (pref[plan[2, s]] * plan[3, s].astype(F32)).astype(BF)
             return carry
 
         lax.fori_loop(0, NSUB, body, 0)
@@ -337,7 +353,7 @@
     return pl.pallas_call(
         gather_kernel,
         out_shape=jax.ShapeDtypeStruct((STAGES, NSUB, 2 * SG, NL), BF),
-        in_specs=[any_spec, any_spec, any_spec, vmem, smem, smem, smem, smem],
+        in_specs=[any_spec, any_spec, any_spec, vmem, smem],
         out_specs=vmem,
         scratch_shapes=[
             *[pltpu.VMEM((NB, CPS, 2 * POL, BLK), BF)] * STAGES,
@@ -361,37 +377,37 @@
             collective_id=0, has_side_effects=True, vmem_limit_bytes=60 * 2**20
         ),
         name="turn_grid_share",
-    )(vis, w_index, offsets, table, *plan)
+    )(vis, w_index, offsets, table, plan)
 
 
 XT = 256
 NT = FX // XT
-
-
-def image_kernel(grids, row_tab, e_cos, e_sin, w_cos, w_sin, keep, out, z, col, edge, cur):
+KH = NSUB * SG
+KQ = 128
+
+
+def image_kernel(rows_s, count_s, grids, row_tab, base, cells, spin, shift, out, z, col, edge, cur):
     step = pl.program_id(0)
-    kblk = 128
-
-    def rotate(q):
-        rows = pl.ds(q * kblk, kblk)
-        c = cur[0, rows]
-        s = cur[1, rows]
-        wc = w_cos[rows]
-        ws = w_sin[rows]
-        cur[0, rows] = c * wc - s * ws
-        cur[1, rows] = s * wc + c * ws
-        return c, s
 
     def fill(width):
-        for q in range(NSUB * SG // kblk):
+        for q in range(KH // KQ):
+            rows = pl.ds(q * KQ, KQ)
+            turn = pl.ds((q % 2) * KQ, KQ)
+            wc = spin[0, turn]
+            ws = spin[1, turn]
+            c = cur[0, rows]
+            s = cur[1, rows]
             for h in range(width // 128):
-                c, s = rotate(q)
-                col[pl.ds(q * 2 * kblk, kblk), pl.ds(h * 128, 128)] = c.astype(BF)
-                col[pl.ds(q * 2 * kblk + kblk, kblk), pl.ds(h * 128, 128)] = (-s).astype(BF)
+                col[pl.ds(q * 2 * KQ, KQ), pl.ds(h * 128, 128)] = c.astype(BF)
+                col[pl.ds(q * 2 * KQ + KQ, KQ), pl.ds(h * 128, 128)] = (-s).astype(BF)
+                c, s = c * wc - s * ws, s * wc + c * ws
+            cur[0, rows] = c
+            cur[1, rows] = s
 
     @pl.when(step == 0)
     def _():
         img_scale = 1.0 / math.sqrt(GROUPS * 65536)
+        facet = lax.axis_index("facet")
 
         def rows4(q, carry):
             for st in range(STAGES):
@@ -405,19 +421,38 @@
                     for p in range(POL):
                         lo = c * POL * SG + p * SG
                         both = jnp.concatenate([o[:, lo : lo + SG] for o in os], axis=1).astype(BF)
-                        base = (st * CPS + c) * POL * FY + p * FY
+                        at = (st * CPS + c) * POL * FY + p * FY
                         lanes0 = pl.ds(pl.multiple_of(q * 256, 128), 128)
                         lanes1 = pl.ds(pl.multiple_of(q * 256 + 128, 128), 128)
-                        z[pl.ds(base, FY), lanes0] = both[:FY]
-                        z[pl.ds(base, FY), lanes1] = both[FY:]
+                        z[pl.ds(at, FY), lanes0] = both[:FY]
+                        z[pl.ds(at, FY), lanes1] = both[FY:]
             return carry
 
         lax.fori_loop(0, NSUB // 4, rows4, 0)
-        cur[0] = e_cos[...]
-        cur[1] = e_sin[...]
+
+        fc = shift[0, facet]
+        fs = shift[1, facet]
+        vc = jnp.concatenate([fc, fc], axis=0)
+        vs = jnp.concatenate([fs, fs], axis=0)
+        cell_c = cells[0] * vc - cells[1] * vs
+        cell_s = cells[1] * vc + cells[0] * vs
+        for g in range(NSUB):
+            rows = pl.ds(g * SG, SG)
+            c = base[0, g : g + 1]
+            s = base[1, g : g + 1]
+            cur[0, rows] = cell_c * c - cell_s * s
+            cur[1, rows] = cell_s * c + cell_c * s
+
         fill(128)
+        before = jnp.maximum(facet - 1, 0)
+        lines = lax.broadcasted_iota(jnp.int32, (FY, MARGIN), 0)
+        used = jnp.where(facet > 0, count_s[before], 0)
+        keep = jnp.zeros((FY, MARGIN), F32)
+        for slot in range(32):
+            row = jnp.where(slot < used, rows_s[before, slot], -1)
+            keep = keep + jnp.where(lines == row, 1.0, 0.0)
         prev = jnp.dot(z[...], col[:, 0:128], preferred_element_type=F32)
-        edge[...] = prev * keep[...]
+        edge[...] = prev.reshape(CH, POL, FY, MARGIN) * keep
 
     fill(XT)
     o = jnp.dot(z[...], col[...], preferred_element_type=F32)
@@ -425,30 +460,35 @@
 
     @pl.when(step == 0)
     def _():
-        out[:, :, :, 0:MARGIN] = out[:, :, :, 0:MARGIN] + edge[...].reshape(CH, POL, FY, MARGIN)
-
-
-def imaged(grids, row_tab, e_cos, e_sin, w_cos, w_sin, keep):
+        out[:, :, :, 0:MARGIN] = out[:, :, :, 0:MARGIN] + edge[...]
+
+
+def imaged(grids, rows_list, counts, *tables):
     def whole(shape):
         return pl.BlockSpec(shape, lambda n: (0,) * len(shape), pipeline_mode=pl.Buffered(1))
 
+    smem = pl.BlockSpec(memory_space=pltpu.SMEM)
     return pl.pallas_call(
         image_kernel,
         grid=(NT,),
         out_shape=jax.ShapeDtypeStruct((CH, POL, FY, FX), F32),
-        in_specs=[
-            whole(a.shape) for a in (grids, row_tab, e_cos, e_sin, w_cos, w_sin, keep)
-        ],
+        in_specs=[smem, smem]
+        + [whole(a.shape) for a in (grids, *tables)],
         out_specs=pl.BlockSpec((CH, POL, FY, XT), lambda n: (0, 0, 0, n)),
         scratch_shapes=[
-            pltpu.VMEM((CH * POL * FY, NSUB * SG * 2), BF),
-            pltpu.VMEM((NSUB * SG * 2, XT), BF),
-            pltpu.VMEM((CH * POL * FY, MARGIN), F32),
-            pltpu.VMEM((2, NSUB * SG, 128), F32),
+            pltpu.VMEM((CH * POL * FY, KH * 2), BF),
+            pltpu.VMEM((KH * 2, XT), BF),
+            pltpu.VMEM((CH, POL, FY, MARGIN), F32),
+            pltpu.VMEM((2, KH, 128), F32),
         ],
         compiler_params=pltpu.CompilerParams(vmem_limit_bytes=60 * 2**20),
         name="facet_image",
-    )(grids, row_tab, e_cos, e_sin, w_cos, w_sin, keep)
+    )(rows_list, counts, grids, *tables)
+
+
+def waves(turns, period):
+    rad = np.mod(turns, period).astype(np.float64) * (2.0 * math.pi / period)
+    return jnp.asarray(np.stack([np.cos(rad), np.sin(rad)]), F32)
 
 
 def row_table():
@@ -467,41 +507,32 @@
 def shards(
     visibilities, w_kernel, w_index, cell_offsets, block_sub, intersection_rows, intersection_count
 ):
-    facet = lax.axis_index("facet")
     vis = visibilities.reshape(visibilities.shape[0], 2 * POL, w_index.shape[1])
-    table = jnp.pad(
-        w_kernel.astype(F32).transpose(1, 2, 0), ((0, 0), (0, 0), (0, 128 - w_kernel.shape[0]))
-    )
+    table = w_kernel.transpose(1, 2, 0)
     grids = gridded(vis, w_index, cell_offsets, table, sort_plan(block_sub))
 
     g = np.arange(NSUB)
     span = NX // SG
     anchor = ((53 * g + 5) % span - span // 2) * SG
-    freq = jnp.asarray((anchor[:, None] + np.arange(SG)[None, :]).reshape(-1, 1), jnp.int32)
-    start = facet * FX - NX // 2 - MARGIN
-    cols = start + jnp.arange(128, dtype=jnp.int32)[None, :]
-    to_rad = 2.0 * math.pi / NX
-    rad = jnp.mod(freq * cols, NX).astype(F32) * to_rad
-    turn = jnp.broadcast_to(jnp.mod(freq * 128, NX).astype(F32) * to_rad, rad.shape)
-
-    before = jnp.maximum(facet - 1, 0)
-    listed = lax.dynamic_index_in_dim(intersection_rows, before, 0, keepdims=False)
-    in_use = lax.dynamic_index_in_dim(intersection_count, before, 0, keepdims=False)
-    slots = jnp.arange(intersection_rows.shape[1], dtype=jnp.int32)
-    lines = jnp.arange(FY, dtype=jnp.int32)
-    row_keep = jnp.sum(
-        ((listed[:, None] == lines[None, :]) & (slots[:, None] < in_use)).astype(F32), axis=0
-    ) * (facet > 0).astype(F32)
-    keep = jnp.broadcast_to(row_keep[None, :, None], (CH * POL, FY, MARGIN)).reshape(-1, MARGIN)
+    freq = (anchor[:, None] + np.arange(SG)[None, :]).reshape(-1, 1)
+    x = -NX // 2 - MARGIN + np.arange(128)[None, :]
+    ones = np.ones((1, 128), np.int64)
+    half = np.arange(16)[:, None]
+    base = waves(anchor[:, None] * x, NX)
+    cells = waves(np.arange(SG)[:, None] * x, NX)
+    spin = waves(freq[: 2 * KQ] * 128 * ones, NX)
+    shift = waves(np.arange(NX // FX)[:, None, None] * FX * half[None] * ones, NX)
+    assert np.all((freq.reshape(-1, 2 * KQ) * 128 - freq[: 2 * KQ].T * 128) % NX == 0)
 
     return imaged(
         grids,
+        intersection_rows,
+        intersection_count,
         jnp.asarray(row_table(), BF),
-        jnp.cos(rad),
-        jnp.sin(rad),
-        jnp.cos(turn),
-        jnp.sin(turn),
-        keep,
+        base,
+        cells,
+        spin,
+        shift,
     )
 
 

time: 120 us -> 107 us (0.89)
  other arithmetic: 8.84 us -> 0 us
  local copies, waits for them, and re-layouts: 5.11 us -> 0 us
    sin x1 -> x0, other arithmetic: 3.9 us -> none  [shards(): jnp.sin(rad)]
    broadcast_in_dim x5 -> x0, local copies, waits for them, and re-layouts: 3.07 us -> none  [the longest x2 2.01 us: shards(): jnp.broadcast_to(jnp.mod(freq * 128, NX).astype(F32) * to_rad, rad.shape)]
    pallas_call x0 -> x1, Pallas kernels: none -> 1.54 us  [sort_plan(): pl.pallas_call(plan_kernel, out_shape=jax.ShapeDtypeStruct((8, 128), jnp....]
    pad x1 -> x0, other arithmetic: 1.29 us -> none  [shards(): jnp.pad(w_kernel.astype(F32).transpose(1, 2, 0), ((0, 0), (0, 0), (0, 128...]
    dynamic_slice x1 -> x0, local copies, waits for them, and re-layouts: 1.25 us -> none  [shards(): lax.dynamic_index_in_dim(intersection_count, before, 0, keepdims=False)]
    convert_element_type x2 -> x0, other arithmetic: 1.2 us -> none  [sort_plan(): return (order, same.astype(F32), last, has.astype(F32))]
where the time goes in v2:
time: 107 us
  Pallas kernels  107 us (100%)
    pallas_call x1, Pallas kernels, gridded(): pl.pallas_call(gather_kernel, out_shape=jax.ShapeDtypeStruct((STAGES, NSU...  83.4 us
    pallas_call x1, Pallas kernels, imaged(): pl.pallas_call(image_kernel, grid=(NT,), out_shape=jax.ShapeDtypeStruct((...  22 us

profile of v2, /device:TPU:0, one launch (start us, length us, event | category | flops | bytes accessed | tf_op | source)
XLA Modules:
  0.0 107.0 jit_solution(12282339630428832986)
XLA Ops:
  0.0 1.5 %sort_plan.1.plan = s32[8,128]{1,0:T(8,128)} custom-call(s32[8,8]{1,0:T(8,128)} %sub.1), custom_call_target="tpu_custom_call" | custom-call | tf_op jit(solution)/shard_map/sort_plan/pallas_call | solution.py:57
  1.5 83.4 %turn_grid_share.1.grids = bf16[2,32,64,256]{3,2,1,0:T(8,128)(2,1)} custom-call(bf16[32,8,4096]{2,1,0:T(8,128)(2,1)} %bitcast.2, s32[8,4096]{1,0:T(8,128)} %widx_h.1, s32[2,8,4096]{2,1,0:T(8,128)} %offs_h.1, bf16[2,8,32]{2,1,0:T(8,128)(2,1)} %bitcast.3, s32[8,128]{1,0:T(8,128)} %sort_plan.1.plan), custom_call_target="tpu_custom_call" | custom-call | tf_op jit(solution)/shard_map/turn_grid_share/pallas_call | solution.py:353
  84.9 22.0 %facet_image.1 = f32[4,4,64,2048]{3,2,1,0:T(8,128)} custom-call(s32[16,32]{1,0:T(8,128)} %rows_s.1, s32[16]{0:T(128)} %count_s.1, bf16[2,32,64,256]{3,2,1,0:T(8,128)(2,1)} %turn_grid_share.1.grids, bf16[32,128,64]{2,1,0:T(8,128)(2,1)} %constant.14.clone.row_tab, f32[2,32,128]{2,1,0:T(8,128)} %constant.10.clone.base, f32[2,32,128]{2,1,0:T(8,128)} %constant.11.clone.cells, ...), custom_call_target="tpu_custom_call" | custom-call | tf_op jit(solution)/shard_map/facet_image/pallas_call | solution.py:471

commit v3 on v2

--- a/solution.py
+++ b/solution.py
@@ -19,7 +19,7 @@
 NB = 64
 CH = 4
 POL = 4
-STAGES = 2
+STAGES = 4
 CPS = CH // STAGES
 NL = CPS * POL * SG
 RING = 4
@@ -326,24 +326,24 @@
             for k in range(1, RING):
                 copies[st, half, 3, k].wait()
 
-    steps = []
+    pending = []
+
+    def advance():
+        for todo in pending:
+            todo.pop(0)()
+        pending[:] = [todo for todo in pending if todo]
+
     for st in range(STAGES):
         turned(st)
         run = jnp.zeros((2 * SG, NL), F32)
-        for piece in range(4):
-            run = grid_part(st, piece * (NB // 4), (piece + 1) * (NB // 4), run)
-            if steps:
-                steps.pop(0)()
+        for piece in range(2):
+            run = grid_part(st, piece * (NB // 2), (piece + 1) * (NB // 2), run)
+            advance()
         emit(st)
         rs1(st)
-        steps += [
-            (lambda st=st: rs2(st)),
-            (lambda st=st: ag1(st)),
-            (lambda st=st: ag2(st)),
-            (lambda st=st: finish(st)),
-        ]
-    for step in steps:
-        step()
+        pending.append([lambda st=st, f=f: f(st) for f in (rs2, ag1, ag2, finish)])
+    while pending:
+        advance()
 
 
 def gridded(vis, w_index, offsets, table, plan):

time: 107 us -> 101 us (0.944)
  Pallas kernels: 107 us -> 101 us
    pallas_call x1, Pallas kernels: 83.4 us -> 77.6 us  [gridded(): pl.pallas_call(gather_kernel, out_shape=jax.ShapeDtypeStruct((STAGES, NSU...]
where the time goes in v3:
time: 101 us
  Pallas kernels  101 us (100%)
    pallas_call x1, Pallas kernels, gridded(): pl.pallas_call(gather_kernel, out_shape=jax.ShapeDtypeStruct((STAGES, NSU...  77.6 us
    pallas_call x1, Pallas kernels, imaged(): pl.pallas_call(image_kernel, grid=(NT,), out_shape=jax.ShapeDtypeStruct((...  22 us

profile of v3, /device:TPU:0, one launch (start us, length us, event | category | flops | bytes accessed | tf_op | source)
XLA Modules:
  0.0 101.1 jit_solution(7455393014394116050)
XLA Ops:
  0.0 1.5 %sort_plan.1.plan = s32[8,128]{1,0:T(8,128)} custom-call(s32[8,8]{1,0:T(8,128)} %sub.1), custom_call_target="tpu_custom_call" | custom-call | tf_op jit(solution)/shard_map/sort_plan/pallas_call | solution.py:57
  1.5 77.6 %turn_grid_share.1.grids = bf16[4,32,64,128]{3,2,1,0:T(8,128)(2,1)} custom-call(bf16[32,8,4096]{2,1,0:T(8,128)(2,1)} %bitcast.2, s32[8,4096]{1,0:T(8,128)} %widx_h.1, s32[2,8,4096]{2,1,0:T(8,128)} %offs_h.1, bf16[2,8,32]{2,1,0:T(8,128)(2,1)} %bitcast.3, s32[8,128]{1,0:T(8,128)} %sort_plan.1.plan), custom_call_target="tpu_custom_call" | custom-call | tf_op jit(solution)/shard_map/turn_grid_share/pallas_call | solution.py:353
  79.1 22.0 %facet_image.1 = f32[4,4,64,2048]{3,2,1,0:T(8,128)} custom-call(s32[16,32]{1,0:T(8,128)} %rows_s.1, s32[16]{0:T(128)} %count_s.1, bf16[4,32,64,128]{3,2,1,0:T(8,128)(2,1)} %turn_grid_share.1.grids, bf16[32,128,64]{2,1,0:T(8,128)(2,1)} %constant.14.clone.row_tab, f32[2,32,128]{2,1,0:T(8,128)} %constant.10.clone.base, f32[2,32,128]{2,1,0:T(8,128)} %constant.11.clone.cells, ...), custom_call_target="tpu_custom_call" | custom-call | tf_op jit(solution)/shard_map/facet_image/pallas_call | solution.py:471

commit v4 on v3

--- a/solution.py
+++ b/solution.py
@@ -233,7 +233,7 @@
             pref[j] = run
             return run
 
-        return lax.fori_loop(lo, hi, body, run, unroll=4)
+        return lax.fori_loop(lo, hi, body, run, unroll=8)
 
     def emit(st):
         def body(s, carry):
@@ -381,15 +381,26 @@
 
 
 XT = 256
-NT = FX // XT
+NT = FX // XT // 2
 KH = NSUB * SG
 KQ = 128
 
 
-def image_kernel(rows_s, count_s, grids, row_tab, base, cells, spin, shift, out, z, col, edge, cur):
+def flipped(x):
+    lanes = 127 - lax.broadcasted_iota(jnp.int32, x.shape, 1)
+    return jnp.take_along_axis(x, lanes, axis=1)
+
+
+def image_kernel(
+    rows_s, count_s, grids, row_tab, base, cells, spin, centre, out,
+    z_re, z_im, col_c, col_s, cur, buf, sems,
+):
     step = pl.program_id(0)
-
-    def fill(width):
+    slot = lax.rem(step, 2)
+    facet = lax.axis_index("facet")
+    tall = CH * POL * FY
+
+    def fill(blocks):
         for q in range(KH // KQ):
             rows = pl.ds(q * KQ, KQ)
             turn = pl.ds((q % 2) * KQ, KQ)
@@ -397,70 +408,94 @@
             ws = spin[1, turn]
             c = cur[0, rows]
             s = cur[1, rows]
-            for h in range(width // 128):
-                col[pl.ds(q * 2 * KQ, KQ), pl.ds(h * 128, 128)] = c.astype(BF)
-                col[pl.ds(q * 2 * KQ + KQ, KQ), pl.ds(h * 128, 128)] = (-s).astype(BF)
+            for h in range(blocks):
+                col_c[rows, pl.ds(h * 128, 128)] = c.astype(BF)
+                col_s[rows, pl.ds(h * 128, 128)] = s.astype(BF)
                 c, s = c * wc - s * ws, s * wc + c * ws
             cur[0, rows] = c
             cur[1, rows] = s
 
+    def writes(n, at):
+        right = FX // 2 + n * XT
+        left = FX // 2 - XT - n * XT
+        return [
+            pltpu.make_async_copy(
+                buf.at[at, side],
+                out.at[:, :, :, pl.ds(pl.multiple_of(lo, XT), XT)],
+                sems.at[at, side],
+            )
+            for side, lo in ((0, right), (1, left))
+        ]
+
     @pl.when(step == 0)
     def _():
         img_scale = 1.0 / math.sqrt(GROUPS * 65536)
-        facet = lax.axis_index("facet")
 
         def rows4(q, carry):
+            tc = centre[0, facet, q]
+            ts = centre[1, facet, q]
+            lanes = pl.ds(pl.multiple_of(q * 128, 128), 128)
             for st in range(STAGES):
                 os = []
                 for gi in range(4):
                     g = q * 4 + gi
-                    os.append(
-                        jnp.dot(row_tab[g], grids[st, g], preferred_element_type=F32) * img_scale
-                    )
+                    os.append(jnp.dot(row_tab[g], grids[st, g], preferred_element_type=F32))
                 for c in range(CPS):
                     for p in range(POL):
                         lo = c * POL * SG + p * SG
-                        both = jnp.concatenate([o[:, lo : lo + SG] for o in os], axis=1).astype(BF)
+                        both = jnp.concatenate([o[:, lo : lo + SG] for o in os], axis=1)
+                        both = both * img_scale
+                        re, im = both[:FY], both[FY:]
                         at = (st * CPS + c) * POL * FY + p * FY
-                        lanes0 = pl.ds(pl.multiple_of(q * 256, 128), 128)
-                        lanes1 = pl.ds(pl.multiple_of(q * 256 + 128, 128), 128)
-                        z[pl.ds(at, FY), lanes0] = both[:FY]
-                        z[pl.ds(at, FY), lanes1] = both[FY:]
+                        z_re[pl.ds(at, FY), lanes] = (re * tc - im * ts).astype(BF)
+                        z_im[pl.ds(at, FY), lanes] = (re * ts + im * tc).astype(BF)
             return carry
 
         lax.fori_loop(0, NSUB // 4, rows4, 0)
-
-        fc = shift[0, facet]
-        fs = shift[1, facet]
-        vc = jnp.concatenate([fc, fc], axis=0)
-        vs = jnp.concatenate([fs, fs], axis=0)
-        cell_c = cells[0] * vc - cells[1] * vs
-        cell_s = cells[1] * vc + cells[0] * vs
         for g in range(NSUB):
             rows = pl.ds(g * SG, SG)
             c = base[0, g : g + 1]
             s = base[1, g : g + 1]
-            cur[0, rows] = cell_c * c - cell_s * s
-            cur[1, rows] = cell_s * c + cell_c * s
-
-        fill(128)
+            cur[0, rows] = cells[0] * c - cells[1] * s
+            cur[1, rows] = cells[1] * c + cells[0] * s
+
+    fill(XT // 128)
+    even = jnp.dot(z_re[...], col_c[...], preferred_element_type=F32)
+    odd = jnp.dot(z_im[...], col_s[...], preferred_element_type=F32)
+
+    @pl.when(step >= 2)
+    def _():
+        for cp in writes(step - 2, slot):
+            cp.wait()
+
+    buf[slot, 0] = (even - odd).reshape(CH, POL, FY, XT)
+    both = even + odd
+    buf[slot, 1, :, :, :, 0:128] = flipped(both[:, 128:]).reshape(CH, POL, FY, 128)
+    buf[slot, 1, :, :, :, 128:] = flipped(both[:, :128]).reshape(CH, POL, FY, 128)
+
+    @pl.when(step == NT - 1)
+    def _():
+        fill(1)
         before = jnp.maximum(facet - 1, 0)
         lines = lax.broadcasted_iota(jnp.int32, (FY, MARGIN), 0)
         used = jnp.where(facet > 0, count_s[before], 0)
         keep = jnp.zeros((FY, MARGIN), F32)
-        for slot in range(32):
-            row = jnp.where(slot < used, rows_s[before, slot], -1)
+        for i in range(32):
+            row = jnp.where(i < used, rows_s[before, i], -1)
             keep = keep + jnp.where(lines == row, 1.0, 0.0)
-        prev = jnp.dot(z[...], col[:, 0:128], preferred_element_type=F32)
-        edge[...] = prev.reshape(CH, POL, FY, MARGIN) * keep
-
-    fill(XT)
-    o = jnp.dot(z[...], col[...], preferred_element_type=F32)
-    out[...] = o.reshape(CH, POL, FY, XT)
-
-    @pl.when(step == 0)
+        edge = jnp.dot(z_re[...], col_c[:, 0:MARGIN], preferred_element_type=F32) + jnp.dot(
+            z_im[...], col_s[:, 0:MARGIN], preferred_element_type=F32
+        )
+        edge = flipped(edge).reshape(CH, POL, FY, MARGIN) * keep
+        buf[slot, 1, :, :, :, 0:MARGIN] = buf[slot, 1, :, :, :, 0:MARGIN] + edge
+
+    for cp in writes(step, slot):
+        cp.start()
+
+    @pl.when(step == NT - 1)
     def _():
-        out[:, :, :, 0:MARGIN] = out[:, :, :, 0:MARGIN] + edge[...]
+        for cp in writes(step - 1, 1 - slot) + writes(step, slot):
+            cp.wait()
 
 
 def imaged(grids, rows_list, counts, *tables):
@@ -472,14 +507,16 @@
         image_kernel,
         grid=(NT,),
         out_shape=jax.ShapeDtypeStruct((CH, POL, FY, FX), F32),
-        in_specs=[smem, smem]
-        + [whole(a.shape) for a in (grids, *tables)],
-        out_specs=pl.BlockSpec((CH, POL, FY, XT), lambda n: (0, 0, 0, n)),
+        in_specs=[smem, smem] + [whole(a.shape) for a in (grids, *tables)],
+        out_specs=pl.BlockSpec(memory_space=pl.ANY),
         scratch_shapes=[
-            pltpu.VMEM((CH * POL * FY, KH * 2), BF),
-            pltpu.VMEM((KH * 2, XT), BF),
-            pltpu.VMEM((CH, POL, FY, MARGIN), F32),
+            pltpu.VMEM((CH * POL * FY, KH), BF),
+            pltpu.VMEM((CH * POL * FY, KH), BF),
+            pltpu.VMEM((KH, XT), BF),
+            pltpu.VMEM((KH, XT), BF),
             pltpu.VMEM((2, KH, 128), F32),
+            pltpu.VMEM((2, 2, CH, POL, FY, XT), F32),
+            pltpu.SemaphoreType.DMA((2, 2)),
         ],
         compiler_params=pltpu.CompilerParams(vmem_limit_bytes=60 * 2**20),
         name="facet_image",
@@ -515,13 +552,13 @@
     span = NX // SG
     anchor = ((53 * g + 5) % span - span // 2) * SG
     freq = (anchor[:, None] + np.arange(SG)[None, :]).reshape(-1, 1)
-    x = -NX // 2 - MARGIN + np.arange(128)[None, :]
+    twice = 2 * np.arange(128)[None, :] + 1
     ones = np.ones((1, 128), np.int64)
-    half = np.arange(16)[:, None]
-    base = waves(anchor[:, None] * x, NX)
-    cells = waves(np.arange(SG)[:, None] * x, NX)
+    base = waves(anchor[:, None] * twice, 2 * NX)
+    cells = waves(np.arange(SG)[:, None] * twice, 2 * NX)
     spin = waves(freq[: 2 * KQ] * 128 * ones, NX)
-    shift = waves(np.arange(NX // FX)[:, None, None] * FX * half[None] * ones, NX)
+    middle = 2 * (np.arange(NX // FX) * FX - NX // 2) + FX - 1
+    centre = waves(middle[:, None, None, None] * freq.reshape(1, KH // 128, 1, 128), 2 * NX)
     assert np.all((freq.reshape(-1, 2 * KQ) * 128 - freq[: 2 * KQ].T * 128) % NX == 0)
 
     return imaged(
@@ -532,7 +569,7 @@
         base,
         cells,
         spin,
-        shift,
+        centre,
     )
 
 

time: 101 us -> 97.5 us (0.965)
  Pallas kernels: 101 us -> 97.3 us
    pallas_call x1, Pallas kernels: 77.6 us -> 75 us  [gridded(): pl.pallas_call(gather_kernel, out_shape=jax.ShapeDtypeStruct((STAGES, NSU...]
    pallas_call x1, Pallas kernels: 22 us -> 20.7 us  [imaged(): pl.pallas_call(image_kernel, grid=(NT,), out_shape=jax.ShapeDtypeStruct((...]
where the time goes in v4:
time: 97.5 us; the launch traced here: 97.3 us
  Pallas kernels  97.3 us (100%)
    pallas_call x1, Pallas kernels, gridded(): pl.pallas_call(gather_kernel, out_shape=jax.ShapeDtypeStruct((STAGES, NSU...  75 us
    pallas_call x1, Pallas kernels, imaged(): pl.pallas_call(image_kernel, grid=(NT,), out_shape=jax.ShapeDtypeStruct((...  20.7 us

profile of v4, /device:TPU:0, one launch (start us, length us, event | category | flops | bytes accessed | tf_op | source)
XLA Modules:
  0.0 97.3 jit_solution(18219598067625974178)
XLA Ops:
  0.0 1.5 %sort_plan.1.plan = s32[8,128]{1,0:T(8,128)} custom-call(s32[8,8]{1,0:T(8,128)} %sub.1), custom_call_target="tpu_custom_call" | custom-call | tf_op jit(solution)/shard_map/sort_plan/pallas_call | solution.py:57
  1.5 75.0 %turn_grid_share.1.grids = bf16[4,32,64,128]{3,2,1,0:T(8,128)(2,1)} custom-call(bf16[32,8,4096]{2,1,0:T(8,128)(2,1)} %bitcast.2, s32[8,4096]{1,0:T(8,128)} %widx_h.1, s32[2,8,4096]{2,1,0:T(8,128)} %offs_h.1, bf16[2,8,32]{2,1,0:T(8,128)(2,1)} %bitcast.3, s32[8,128]{1,0:T(8,128)} %sort_plan.1.plan), custom_call_target="tpu_custom_call" | custom-call | tf_op jit(solution)/shard_map/turn_grid_share/pallas_call | solution.py:353
  76.6 20.7 %facet_image.1 = f32[4,4,64,2048]{3,2,1,0:T(8,128)} custom-call(s32[16,32]{1,0:T(8,128)} %rows_s.1, s32[16]{0:T(128)} %count_s.1, bf16[4,32,64,128]{3,2,1,0:T(8,128)(2,1)} %turn_grid_share.1.grids, bf16[32,128,64]{2,1,0:T(8,128)(2,1)} %constant.14.clone.row_tab, f32[2,32,128]{2,1,0:T(8,128)} %constant.10.clone.base, f32[2,32,128]{2,1,0:T(8,128)} %constant.11.clone.cells, ...), custom_call_target="tpu_custom_call" | custom-call | tf_op jit(solution)/shard_map/facet_image/pallas_call | solution.py:506
